TPU v7x, 32 devices: a whole 2x2x4 slice. The times are simulated.
32 devices in a mesh: task: 4 (over x, core), tensor: 4 (over z), dp: 2 (over y).
Axes of the slice: x: 2, y: 2, z: 4, core: 2. Of those that a mesh axis runs over, the one named last changes fastest.
Arguments:
- hidden: bfloat16 [1024, 4608], P(('task', 'dp')), may hold values from -6 to 6
- pre_gain: float32 [4608], replicated, may hold values from 0.1 to 1.9
- base_query: bfloat16 [4608, 512], P('dp', 'tensor'), may hold values from -0.09375 to 0.09375
- base_keyval: bfloat16 [2, 4608, 256], P(None, 'dp', 'tensor'), may hold values from -0.09375 to 0.09375
- base_output: bfloat16 [512, 4608], P('tensor', 'dp'), may hold values from -0.25 to 0.25
- delta_query: bfloat16 [4, 4608, 512], P('task', 'dp', 'tensor'), may hold values from -0.046875 to 0.046875
- delta_keyval: bfloat16 [4, 2, 4608, 256], P('task', None, 'dp', 'tensor'), may hold values from -0.046875 to 0.046875
- delta_output: bfloat16 [4, 512, 4608], P('task', 'tensor', 'dp'), may hold values from -0.125 to 0.125
- trim_query: int32 [4, 72, 8], P('task', 'dp', 'tensor'), may hold values 0 or 1
- trim_keyval: int32 [4, 2, 72, 4], P('task', None, 'dp', 'tensor'), may hold values 0 or 1
- trim_output: int32 [4, 8, 72], P('task', 'tensor', 'dp'), may hold values 0 or 1
- sign_query: int32 [72, 8], P('dp', 'tensor'), may hold values from 0 to 1
- sign_keyval: int32 [2, 72, 4], P(None, 'dp', 'tensor'), may hold values from 0 to 1
- sign_output: int32 [8, 72], P('tensor', 'dp'), may hold values from 0 to 1
- post_gain: float32 [4608], replicated, may hold values from 0.1 to 1.9
- final_gain: float32 [4608], replicated, may hold values from 0.1 to 1.9
- unembedding: bfloat16 [28672, 4608], P(('task', 'tensor', 'dp')), may hold values from -0.375 to 0.375
- targets: int32 [1024], replicated, may hold values from 0 to 28671
- loss_mask: int32 [1024], replicated, may hold values 0 or 1
Outputs:
- token_loss: float32 [1024], P(('task', 'dp'))
- summary: float32 [2], replicated
All inputs are finite; a program needn't handle non-finite values. No bound on the sum of `trim_query` or of `trim_keyval` or of `trim_output` on one device may be relied on, other than what follows from the above.
Results may differ from a plain program's by a relative error of at most 0.0045.
Values may be sent and summed in bfloat16 or wider, within the bound.
No kernel may reach another device: no remote copies, remote signals or barrier semaphores. Data moves between devices by JAX's collectives and lax.ppermute only.
A program may use at most 128 MiB of HBM per device.

v0:
```python
import jax
import jax.numpy as jnp
from jax import lax
from jax.sharding import PartitionSpec as P

BLK = 64
EPSILON = 1e-06
QUERY_SCALE = 1.0 / 12.0
ROPE_BASE = 10000.0
SCORE_CAP = 50.0
LOGIT_CAP = 30.0


def from_partner(block, axis, bit):
    count = lax.axis_size(axis)
    route = []
    for low in range(count):
        high = low | 1 << bit
        if high != low and high < count:
            route += [(low, high), (high, low)]
    return lax.ppermute(block, axis, route)


def trim_delta(deltas, trim_bits, sign_bits):
    layout = deltas.shape
    row_blocks = layout[-2] // BLK
    col_blocks = layout[-1] // BLK
    blocks = deltas.reshape(layout[:-2] + (row_blocks, BLK, col_blocks, BLK))
    wanted = (2 * sign_bits - 1).astype(jnp.float32)[..., :, None, :, None]
    keeping = (trim_bits[..., :, None, :, None] == 1) & (
        jnp.sign(blocks.astype(jnp.float32)) == wanted
    )
    return jnp.where(keeping, blocks, jnp.zeros_like(blocks)).reshape(layout)


def finish_merge(base_part, totals, counts):
    return (base_part.astype(jnp.float32) + totals / jnp.maximum(counts, 1.0)).astype(jnp.bfloat16)


def merge_every(base_part, gathered):
    totals = jnp.sum(gathered.astype(jnp.float32), axis=0)
    counts = jnp.sum((gathered != 0).astype(jnp.float32), axis=0)
    return finish_merge(base_part, totals, counts)


def rms_norm(values, gain):
    scale = lax.rsqrt(jnp.mean(values * values, axis=-1, keepdims=True) + EPSILON)
    return values * scale * gain


def rotate(values, angles):
    half_width = values.shape[-1] // 2
    first = values[..., :half_width]
    second = values[..., half_width:]
    cosine = jnp.cos(angles)
    sine = jnp.sin(angles)
    return jnp.concatenate(
        [first * cosine - second * sine, second * cosine + first * sine], axis=-1
    )


def on_device(
    hidden,
    pre_gain,
    base_query,
    base_keyval,
    base_output,
    delta_query,
    delta_keyval,
    delta_output,
    trim_query,
    trim_keyval,
    trim_output,
    sign_query,
    sign_keyval,
    sign_output,
    post_gain,
    final_gain,
    unembedding,
    targets,
    loss_mask,
):
    kept_query = trim_delta(delta_query, trim_query, sign_query)
    kept_keyval = trim_delta(delta_keyval, trim_keyval, sign_keyval)
    kept_output = trim_delta(delta_output, trim_output, sign_output)
    gathered = (
        lax.all_gather(kept_query, "task", axis=0, tiled=True),
        lax.all_gather(kept_keyval, "task", axis=0, tiled=True),
        lax.all_gather(kept_output, "task", axis=0, tiled=True),
    )
    halves = (
        merge_every(base_query, gathered[0]),
        merge_every(base_keyval, gathered[1]),
        merge_every(base_output, gathered[2]),
    )
    merged_query, merged_keyval, merged_output = (
        lax.all_gather(halves[0], "dp", axis=0, tiled=True),
        lax.all_gather(halves[1], "dp", axis=1, tiled=True),
        lax.all_gather(halves[2], "dp", axis=1, tiled=True),
    )
    residual = hidden.astype(jnp.float32)
    normed = rms_norm(residual, pre_gain).astype(jnp.bfloat16)
    row_count = residual.shape[0]
    group_index = lax.axis_index(("task", "dp"))
    query_positions = group_index * row_count + jnp.arange(row_count, dtype=jnp.int32)
    head_width = merged_query.shape[1]
    frequencies = jnp.exp(
        -jnp.log(ROPE_BASE)
        * 2.0
        * jnp.arange(head_width // 2, dtype=jnp.int32).astype(jnp.float32)
        / head_width
    )
    angles = query_positions.astype(jnp.float32)[:, None] * frequencies[None, :]
    queries = jnp.dot(normed, merged_query, preferred_element_type=jnp.float32)
    queries = (rotate(queries, angles) * QUERY_SCALE).astype(jnp.bfloat16)
    key_half = jnp.dot(normed, merged_keyval[0], preferred_element_type=jnp.float32)
    value_half = jnp.dot(normed, merged_keyval[1], preferred_element_type=jnp.float32)
    other_key, other_value = (
        from_partner(key_half.astype(jnp.bfloat16), "tensor", 0).astype(key_half.dtype),
        from_partner(value_half.astype(jnp.bfloat16), "tensor", 0).astype(value_half.dtype),
    )
    is_lower = lax.axis_index("tensor") % 2 == 0
    keys_full = jnp.where(
        is_lower,
        jnp.concatenate([key_half, other_key], axis=1),
        jnp.concatenate([other_key, key_half], axis=1),
    )
    values_full = jnp.where(
        is_lower,
        jnp.concatenate([value_half, other_value], axis=1),
        jnp.concatenate([other_value, value_half], axis=1),
    )
    keys_full = rotate(keys_full, angles).astype(jnp.bfloat16)
    values_full = values_full.astype(jnp.bfloat16)
    key_piece = lax.all_gather(keys_full, ("task", "dp"), axis=0, tiled=True)
    value_piece = lax.all_gather(values_full, ("task", "dp"), axis=0, tiled=True)
    scores = lax.dot_general(
        queries, key_piece, (((1,), (1,)), ((), ())), preferred_element_type=jnp.float32
    )
    capped = SCORE_CAP * jnp.tanh(scores / SCORE_CAP)
    key_positions = jnp.arange(key_piece.shape[0], dtype=jnp.int32)
    allowed = key_positions[None, :] <= query_positions[:, None]
    weights = jnp.where(allowed, jnp.exp(capped), 0.0)
    numerator = jnp.dot(
        weights.astype(jnp.bfloat16), value_piece, preferred_element_type=jnp.float32
    )
    denominator = jnp.sum(weights, axis=1)
    numerator, denominator = (numerator, denominator)
    attention = (numerator / denominator[:, None]).astype(jnp.bfloat16)
    partial_value = jnp.dot(attention, merged_output, preferred_element_type=jnp.float32)
    task_count = lax.axis_size("task")
    tensor_count = lax.axis_size("tensor")
    dp_count = lax.axis_size("dp")
    span_rows = row_count // tensor_count
    share_rows = lax.psum_scatter(
        partial_value.astype(jnp.bfloat16), "tensor", scatter_dimension=0, tiled=True
    ).astype(jnp.float32)
    own_stream = lax.dynamic_slice_in_dim(
        residual, lax.axis_index("tensor") * span_rows, span_rows, 0
    )
    stream = own_stream + rms_norm(share_rows, post_gain)
    final = rms_norm(stream, final_gain).astype(jnp.bfloat16)
    every_rows = lax.all_gather(final, ("task", "tensor", "dp"), axis=0, tiled=True)
    ordered_targets = jnp.transpose(
        targets.reshape(task_count, dp_count, tensor_count, span_rows), (0, 2, 1, 3)
    ).reshape(-1)
    ordered_mask = jnp.transpose(
        loss_mask.reshape(task_count, dp_count, tensor_count, span_rows), (0, 2, 1, 3)
    ).reshape(-1)
    logits = lax.dot_general(
        every_rows, unembedding, (((1,), (1,)), ((), ())), preferred_element_type=jnp.float32
    )
    capped = LOGIT_CAP * jnp.tanh(logits / LOGIT_CAP)
    vocab_ids = lax.axis_index(("task", "tensor", "dp")) * unembedding.shape[0] + jnp.arange(
        unembedding.shape[0], dtype=jnp.int32
    )
    local_sumexp = jnp.sum(jnp.exp(capped), axis=1)
    local_target = jnp.sum(
        jnp.where(ordered_targets[:, None] == vocab_ids[None, :], capped, 0.0), axis=1
    )
    sumexp, target_logit = lax.psum((local_sumexp, local_target), ("task", "tensor", "dp"))
    counted = ordered_mask.astype(jnp.float32)
    losses = (jnp.log(sumexp) - target_logit) * counted
    summary = jnp.stack([jnp.sum(losses), jnp.sum(counted)])
    losses = jnp.transpose(
        losses.reshape(task_count, tensor_count, dp_count, span_rows), (0, 2, 1, 3)
    ).reshape(-1)
    own_losses = lax.dynamic_slice_in_dim(losses, group_index * row_count, row_count, 0)
    return (own_losses, summary)


def solution(mesh):
    return jax.shard_map(
        on_device,
        mesh=mesh,
        in_specs=(
            P(("task", "dp"), None),
            P(),
            P("dp", "tensor"),
            P(None, "dp", "tensor"),
            P("tensor", "dp"),
            P("task", "dp", "tensor"),
            P("task", None, "dp", "tensor"),
            P("task", "tensor", "dp"),
            P("task", "dp", "tensor"),
            P("task", None, "dp", "tensor"),
            P("task", "tensor", "dp"),
            P("dp", "tensor"),
            P(None, "dp", "tensor"),
            P("tensor", "dp"),
            P(),
            P(),
            P(("task", "tensor", "dp"), None),
            P(),
            P(),
        ),
        out_specs=(P(("task", "dp")), P()),
        check_vma=False,
    )
```

profile of v0, /device:TPU:0, one launch (start us, length us, event | category | flops | bytes accessed | tf_op | source)
XLA Modules:
  0.0 354.9 jit_solution(13832820005379422890)
XLA Ops:
  7.2 0.7 add_convert_fusion.4
  8.0 0.1 eq.117
  8.1 0.7 broadcast_compare_fusion
  8.8 0.1 and.54
  8.9 2.6 fusion.7
  11.7 0.1 copy.38
  11.8 0.7 eq.108
  12.5 1.3 eq.109
  13.8 0.4 copy.39
  14.1 0.3 copy-done.15
  14.4 0.2 and.49
  14.7 0.8 and.50
  15.5 0.2 copy.37
  15.7 0.6 fusion.5
  16.3 1.1 copy.41
  17.5 0.1 copy.44
  17.6 0.7 eq.123
  18.3 1.3 eq.124
  19.6 0.4 copy.45
  20.0 0.3 copy-done.16
  20.3 0.2 and.57
  20.5 0.8 and.58
  21.3 0.1 copy-done.6
  21.4 1.4 fusion.9
  22.8 1.1 copy.36
  24.0 0.3 multiply_reduce_fusion
  24.3 14.2 %all-gather.12.cloned.1.call-done = bf16[4,2,2304,64]{2,3,1,0:T(8,128)(2,1)} async-done(((bf16[1,2,2304,64]{2,3,1,0:T(8,128)(2,1)}), bf16[4,2,2304,64]{2,3,1,0:T(8,128)(2,1)}) %all-gather.12.cloned.1.call-update) | async-done | bytes 2359312 | tf_op jit(solution)/shard_map/all_gather | solution.py:88
  38.5 3.6 %convert_reduce_fusion.2 = (f32[2,2304,64]{1,2,0:T(8,128)S(1)}, f32[2,2304,64]{1,2,0:T(8,128)S(1)}) fusion(bf16[4,2,2304,64]{2,3,1,0:T(8,128)(2,1)} %all-gather.12.cloned.1.call-done), kind=kLoop, calls=%fused_computation.3 | loop fusion | flops 5308416 | bytes 4718592 | tf_op jit(solution)/shard_map/reduce_sum | solution.py:42
  42.2 1.1 add_convert_fusion.1
  43.3 0.2 all-gather.10.cloned.1.call-start
  43.5 20.6 %all-gather.8.cloned.1.call-done = bf16[4,2304,128]{2,1,0:T(8,128)(2,1)} async-done(((bf16[1,2304,128]{2,1,0:T(8,128)(2,1)}), bf16[4,2304,128]{2,1,0:T(8,128)(2,1)}) %all-gather.8.cloned.1.call-update) | async-done | bytes 2359312 | tf_op jit(solution)/shard_map/all_gather | solution.py:87
  64.2 4.6 %convert_reduce_fusion.4 = (f32[2304,128]{1,0:T(8,128)}, f32[2304,128]{1,0:T(8,128)S(1)}) fusion(bf16[4,2304,128]{2,1,0:T(8,128)(2,1)} %all-gather.8.cloned.1.call-done), kind=kLoop, calls=%fused_computation.5 | loop fusion | flops 5308416 | bytes 4718592 | tf_op jit(solution)/shard_map/reduce_sum | solution.py:42
  68.8 0.4 copy.50
  69.1 1.6 copy.51
  70.8 2.2 add_convert_fusion.2
  73.1 16.7 %all-gather.16.cloned.1.call-done = bf16[4,128,2304]{2,1,0:T(8,128)(2,1)} async-done(((bf16[1,128,2304]{2,1,0:T(8,128)(2,1)}), bf16[4,128,2304]{2,1,0:T(8,128)(2,1)}) %all-gather.16.cloned.1.call-update) | async-done | bytes 2359312 | tf_op jit(solution)/shard_map/all_gather | solution.py:89
  89.8 3.6 %convert_reduce_fusion = (f32[128,2304]{1,0:T(8,128)S(1)}, f32[128,2304]{1,0:T(8,128)S(1)}) fusion(bf16[4,128,2304]{2,1,0:T(8,128)(2,1)} %all-gather.16.cloned.1.call-done), kind=kLoop, calls=%fused_computation.1 | loop fusion | flops 5308416 | bytes 4718592 | tf_op jit(solution)/shard_map/reduce_sum | solution.py:42
  93.5 1.1 add_convert_fusion
  94.6 19.4 %all-gather.14.cloned.1.call-done = bf16[2,4608,64]{1,2,0:T(8,128)(2,1)} async-done(((bf16[2,2304,64]{1,2,0:T(8,128)(2,1)}), bf16[2,4608,64]{1,2,0:T(8,128)(2,1)}) %all-gather.14.cloned.1.call-update) | async-done | bytes 1179664 | tf_op jit(solution)/shard_map/all_gather | solution.py:98
  114.0 1.8 fusion.42
  115.8 1.6 collective-permute-start
  117.3 0.6 fusion.14
  117.9 0.6 collective-permute-start.1
  118.5 19.6 %all-gather.10.cloned.1.call-done = bf16[4608,128]{0,1:T(8,128)(2,1)} async-done(((bf16[2304,128]{0,1:T(8,128)(2,1)}), bf16[4608,128]{0,1:T(8,128)(2,1)}) %all-gather.10.cloned.1.call-update) | async-done | bytes 1179664 | tf_op jit(solution)/shard_map/all_gather | solution.py:97
  138.2 1.8 fusion.40
  140.0 0.2 fusion.28
  140.3 16.4 %all_gather.31 = bf16[1024,128]{0,1:T(8,128)(2,1)S(1)} all-gather(bf16[128,128]{0,1:T(8,128)(2,1)S(1)} %pad_maximum_fusion), channel_id=1, replica_groups=mesh['task'=4,'tensor'=4,'dp'=2] {'task','dp'}, dimensions={0}, use_global_device_ids=true | all-gather | bytes 294912 | tf_op jit(solution)/shard_map/all_gather | solution.py:135
  156.7 17.9 %all_gather.32 = bf16[1024,128]{0,1:T(8,128)(2,1)S(1)} all-gather(bf16[128,128]{0,1:T(8,128)(2,1)S(1)} %fusion.19), channel_id=1, replica_groups=mesh['task'=4,'tensor'=4,'dp'=2] {'task','dp'}, dimensions={0}, use_global_device_ids=true | all-gather | bytes 294912 | tf_op jit(solution)/shard_map/all_gather | solution.py:136
  174.6 0.4 fusion.43
  175.1 3.1 convolution_convert_fusion
  178.2 0.2 convert_element_type.132
  178.5 29.2 %reduce-scatter.2.cloned.1.call-done = bf16[32,4608]{1,0:T(8,128)(2,1)} async-done(((bf16[128,4608]{1,0:T(8,128)(2,1)}), bf16[32,4608]{1,0:T(8,128)(2,1)}) %reduce-scatter.2.cloned.1.call-update) | async-done | bytes 294928 | tf_op jit(solution)/shard_map/reduce_scatter | solution.py:155
  207.7 1.2 fusion.11
  208.9 1.3 multiply_reduce_fusion.1
  210.2 0.9 multiply_convert_fusion.1
  211.2 0.1 eq.126
  211.4 0.1 convert_element_type.168
  211.5 0.6 convert_reduce_fusion.6
  212.1 79.2 %all-gather.20.cloned.1.call-done = bf16[1024,4608]{1,0:T(8,128)(2,1)} async-done(((bf16[32,4608]{1,0:T(8,128)(2,1)}), bf16[1024,4608]{1,0:T(8,128)(2,1)}) %all-gather.20.cloned.1.call-update) | async-done | bytes 9437200 | tf_op jit(solution)/shard_map/all_gather | solution.py:163
  291.4 14.4 %exponential_reduce_fusion = (f32[1024]{0:T(1024)S(1)}, f32[1024]{0:T(1024)S(1)}) fusion(s32[896]{0:T(1024)S(1)} %iota_add_fusion, s32[1024]{0:T(1024)S(1)} %eq.126, bf16[1024,4608]{1,0:T(8,128)(2,1)} %all-gather.20.cloned.1.call-done, bf16[896,4608]{1,0:T(8,128)(2,1)} %param.35), kind=kOutput, calls=%fused_computation.8 | convolution fusion | flops 8461219840 | bytes 17710592 | tf_op jit(solution)/shard_map/dot_general | solution.py:170
  305.7 39.1 %all-reduce = (f32[1024]{0:T(1024)S(1)}, f32[1024]{0:T(1024)S(1)}) all-reduce(f32[1024]{0:T(1024)S(1)} %get-tuple-element.3, f32[1024]{0:T(1024)S(1)} %get-tuple-element.2), channel_id=1, replica_groups=mesh['task'=4,'tensor'=4,'dp'=2] {'task','tensor','dp'}, use_global_device_ids=true, to_apply=%region_14.15 | all-reduce | flops 2048 | bytes 16384 | tf_op jit(solution)/shard_map/psum | solution.py:181
  344.8 0.6 fusion.41
  345.6 0.6 dynamic_slice.7
  346.2 1.8 pad_maximum_fusion.1
  (75 shorter events, 1.2 us)
Async XLA Ops:
  7.2 4.5 %copy-start.11 = (s32[36,2]{0,1:T(2,128)S(1)}, s32[36,2]{0,1:T(2,128)}, u32[]{:S(2)}) copy-start(s32[36,2]{0,1:T(2,128)} %param.30) | copy-start | bytes 868
  7.2 31.4 %all-gather.12.cloned.1.call-start = ((), (), s32[]{:S(2)}) async-start(), calls=%async_computation.3 | async-start | bytes 2949120 | tf_op jit(solution)/shard_map/all_gather | solution.py:88
  11.6 52.6 %all-gather.8.cloned.1.call-start = ((), (), s32[]{:S(2)}) async-start(), calls=%async_computation.1 | async-start | bytes 2949120 | tf_op jit(solution)/shard_map/all_gather | solution.py:87
  13.7 0.7 copy-start.15
  14.4 1.1 copy-start.4
  16.3 1.2 copy-start.12
  17.4 72.4 %all-gather.16.cloned.1.call-start = ((), (), s32[]{:S(2)}) async-start(), calls=%async_computation.5 | async-start | bytes 2949120 | tf_op jit(solution)/shard_map/all_gather | solution.py:89
  19.6 0.7 copy-start.16
  20.3 1.1 copy-start.6
  21.4 1.5 copy-start.5
  22.7 1.3 copy-start
  22.7 91.3 %all-gather.14.cloned.1.call-start = ((), (), s32[]{:S(2)}) async-start(), calls=%async_computation.4 | async-start | bytes 1769472 | tf_op jit(solution)/shard_map/all_gather | solution.py:98
  24.3 17.9 %copy-start.2 = (bf16[2,2304,64]{1,2,0:T(8,128)(2,1)S(1)}, bf16[2,2304,64]{1,2,0:T(8,128)(2,1)}, u32[]{:S(2)}) copy-start(bf16[2,2304,64]{1,2,0:T(8,128)(2,1)} %param.22) | copy-start | bytes 1769476
  43.3 94.9 %all-gather.10.cloned.1.call-start = ((), (), s32[]{:S(2)}) async-start(), calls=%async_computation.2 | async-start | bytes 1769472 | tf_op jit(solution)/shard_map/all_gather | solution.py:97
  73.0 102.1 %all-gather.18.cloned.1.call-start = ((), (), s32[]{:S(2)}) async-start(), calls=%async_computation.6 | async-start | bytes 1769472 | tf_op jit(solution)/shard_map/all_gather | solution.py:99
  73.1 20.4 %copy-start.3 = (bf16[128,2304]{1,0:T(8,128)(2,1)S(1)}, bf16[128,2304]{1,0:T(8,128)(2,1)}, u32[]{:S(2)}) copy-start(bf16[128,2304]{1,0:T(8,128)(2,1)} %param.23) | copy-start | bytes 1769476
  93.5 20.5 %copy-start.14 = (f32[4608]{0:T(1024)S(1)}, f32[4608]{0:T(1024)}, u32[]{:S(2)}) copy-start(f32[4608]{0:T(1024)} %param.20) | copy-start | bytes 55300
  94.6 113.1 %reduce-scatter.2.cloned.1.call-start = ((), (), s32[]{:S(2)}) async-start(), calls=%async_computation.7 | async-start | bytes 1474560 | tf_op jit(solution)/shard_map/reduce_scatter | solution.py:155
  114.0 3.3 copy-start.13
  115.8 24.2 %collective-permute-start = (bf16[128,64]{0,1:T(8,128)(2,1)S(1)}, bf16[128,64]{0,1:T(8,128)(2,1)S(1)}, u32[]{:S(2)}, u32[]{:S(2)}) collective-permute-start(bf16[128,64]{0,1:T(8,128)(2,1)S(1)} %get-tuple-element.20), channel_id=1, source_target_pairs={{0,2},{2,0},{4,6},{6,4},{1,3},{3,1},{5,7},{7,5},{8,10},{10,8},{12,... | collective-permute-start | bytes 49160 | tf_op jit(solution)/shard_map/ppermute | solution.py:21
  117.9 38.8 %collective-permute-start.1 = (bf16[128,64]{0,1:T(8,128)(2,1)S(1)}, bf16[128,64]{0,1:T(8,128)(2,1)S(1)}, u32[]{:S(2)}, u32[]{:S(2)}) collective-permute-start(bf16[128,64]{0,1:T(8,128)(2,1)S(1)} %fusion.14), channel_id=1, source_target_pairs={{0,2},{2,0},{4,6},{6,4},{1,3},{3,1},{5,7},{7,5},{8,10},{10,8},{12,... | collective-permute-start | bytes 49160 | tf_op jit(solution)/shard_map/ppermute | solution.py:21
  178.2 113.2 %all-gather.20.cloned.1.call-start = ((), (), s32[]{:S(2)}) async-start(), calls=%async_computation.8 | async-start | bytes 9732096 | tf_op jit(solution)/shard_map/all_gather | solution.py:163
  178.5 31.7 %copy-start.7 = (f32[4608]{0:T(1024)S(1)}, f32[4608]{0:T(1024)}, u32[]{:S(2)}) copy-start(f32[4608]{0:T(1024)} %param.33) | copy-start | bytes 55300
  178.5 31.7 %copy-start.8 = (f32[4608]{0:T(1024)S(1)}, f32[4608]{0:T(1024)}, u32[]{:S(2)}) copy-start(f32[4608]{0:T(1024)} %param.34) | copy-start | bytes 55300
  207.7 2.5 copy-start.1
  208.9 2.3 copy-start.10
  208.9 2.5 copy-start.9
Sparse Core Ops, SparseCore 0:
  11.7 26.7 all-gather.11
  40.1 24.0 all-gather.7
  65.7 24.0 all-gather.15
  91.2 22.7 all-gather.13
  115.4 22.7 all-gather.9
  139.6 24.4 all-gather.17
  178.3 29.3 reduce-scatter.1
  211.3 80.0 all-gather.19
where the time goes:
time: 356 us; the launch traced here: 355 us
  waiting for transfers between devices  199 us (56%)
  blocking collectives  73.5 us (21%)
  other arithmetic  29.4 us (8%)
  matrix products  22 us (6%)
  between operations  14.6 us (4%)
  local copies, waits for them, and re-layouts  13.6 us (4%)
    all_gather x1, waiting for transfers between devices, on_device(): lax.all_gather(final, ('task', 'tensor', 'dp'), axis=0, tiled=True)  79.2 us
    psum x1, blocking collectives, on_device(): lax.psum((local_sumexp, local_target), ('task', 'tensor', 'dp'))  39.1 us
    reduce_scatter x1, waiting for transfers between devices, on_device(): lax.psum_scatter(partial_value.astype(jnp.bfloat16), 'tensor', scatter_di...  29.2 us
    all_gather x1, waiting for transfers between devices, on_device(): lax.all_gather(kept_query, 'task', axis=0, tiled=True)  20.6 us
    all_gather x1, waiting for transfers between devices, on_device(): lax.all_gather(halves[0], 'dp', axis=0, tiled=True)  19.6 us
    all_gather x1, waiting for transfers between devices, on_device(): lax.all_gather(halves[1], 'dp', axis=1, tiled=True)  19.4 us
    all_gather x1, blocking collectives, on_device(): lax.all_gather(values_full, ('task', 'dp'), axis=0, tiled=True)  17.9 us
    all_gather x1, waiting for transfers between devices, on_device(): lax.all_gather(kept_output, 'task', axis=0, tiled=True)  16.7 us
  transfers between devices with their start and end apart: 10, of which 7 were waited for; matrix products, arithmetic and copies ran while one was open for 10% of the time, Pallas kernels for 0%

commit v1 on v0

--- a/solution.py
+++ b/solution.py
@@ -178,7 +178,9 @@
     local_target = jnp.sum(
         jnp.where(ordered_targets[:, None] == vocab_ids[None, :], capped, 0.0), axis=1
     )
-    sumexp, target_logit = lax.psum((local_sumexp, local_target), ("task", "tensor", "dp"))
+    sumexp, target_logit = lax.psum(
+        lax.psum((local_sumexp, local_target), ("tensor", "dp")), "task"
+    )
     counted = ordered_mask.astype(jnp.float32)
     losses = (jnp.log(sumexp) - target_logit) * counted
     summary = jnp.stack([jnp.sum(losses), jnp.sum(counted)])

time: 356 us -> 343 us (0.963)
  blocking collectives: 73.5 us -> 60.6 us
    psum x1 -> x2, blocking collectives: 39.1 us -> 26.3 us  [the longest x1 20.1 us: on_device(): lax.psum((local_sumexp, local_target), ('tensor', 'dp'))]
  transfers between devices with their start and end apart: 10 -> 10, of which waited for: 7 -> 7; matrix products, arithmetic and copies ran while one was open for 10% -> 11% of each run, Pallas kernels for 0% -> 0%
where the time goes in v1:
time: 343 us; the launch traced here: 342 us
  waiting for transfers between devices  199 us (58%)
  blocking collectives  60.6 us (18%)
  other arithmetic  29.5 us (9%)
  matrix products  22 us (6%)
  between operations  14.6 us (4%)
  local copies, waits for them, and re-layouts  13.6 us (4%)
    all_gather x1, waiting for transfers between devices, on_device(): lax.all_gather(final, ('task', 'tensor', 'dp'), axis=0, tiled=True)  79.2 us
    reduce_scatter x1, waiting for transfers between devices, on_device(): lax.psum_scatter(partial_value.astype(jnp.bfloat16), 'tensor', scatter_di...  29.1 us
    all_gather x1, waiting for transfers between devices, on_device(): lax.all_gather(kept_query, 'task', axis=0, tiled=True)  20.7 us
    psum x1, blocking collectives, on_device(): lax.psum((local_sumexp, local_target), ('tensor', 'dp'))  20.1 us
    all_gather x1, waiting for transfers between devices, on_device(): lax.all_gather(halves[0], 'dp', axis=0, tiled=True)  19.6 us
    all_gather x1, waiting for transfers between devices, on_device(): lax.all_gather(halves[1], 'dp', axis=1, tiled=True)  19.3 us
    all_gather x1, blocking collectives, on_device(): lax.all_gather(values_full, ('task', 'dp'), axis=0, tiled=True)  17.9 us
    all_gather x1, waiting for transfers between devices, on_device(): lax.all_gather(kept_output, 'task', axis=0, tiled=True)  16.7 us
  transfers between devices with their start and end apart: 10, of which 7 were waited for; matrix products, arithmetic and copies ran while one was open for 11% of the time, Pallas kernels for 0%

profile of v1, /device:TPU:0, one launch (start us, length us, event | category | flops | bytes accessed | tf_op | source)
XLA Modules:
  0.0 342.0 jit_solution(7970432330395294881)
XLA Ops:
  7.2 0.7 add_convert_fusion.4
  8.0 0.1 eq.117
  8.1 0.7 broadcast_compare_fusion
  8.8 0.1 and.54
  8.9 2.6 fusion.7
  11.7 0.1 copy.38
  11.8 0.7 eq.108
  12.4 1.3 eq.109
  13.7 0.4 copy.39
  14.1 0.3 copy-done.15
  14.4 0.2 and.49
  14.7 0.8 and.50
  15.5 0.2 copy.37
  15.7 0.6 fusion.5
  16.3 1.1 copy.41
  17.5 0.1 copy.44
  17.6 0.7 eq.123
  18.3 1.3 eq.124
  19.6 0.4 copy.45
  20.0 0.3 copy-done.16
  20.3 0.2 and.57
  20.5 0.8 and.58
  21.4 1.4 fusion.9
  22.8 1.2 copy.36
  24.0 0.3 multiply_reduce_fusion
  24.3 14.2 %all-gather.12.cloned.1.call-done = bf16[4,2,2304,64]{2,3,1,0:T(8,128)(2,1)} async-done(((bf16[1,2,2304,64]{2,3,1,0:T(8,128)(2,1)}), bf16[4,2,2304,64]{2,3,1,0:T(8,128)(2,1)}) %all-gather.12.cloned.1.call-update) | async-done | bytes 2359312 | tf_op jit(solution)/shard_map/all_gather | solution.py:88
  38.5 3.6 %convert_reduce_fusion.2 = (f32[2,2304,64]{1,2,0:T(8,128)S(1)}, f32[2,2304,64]{1,2,0:T(8,128)S(1)}) fusion(bf16[4,2,2304,64]{2,3,1,0:T(8,128)(2,1)} %all-gather.12.cloned.1.call-done), kind=kLoop, calls=%fused_computation.3 | loop fusion | flops 5308416 | bytes 4718592 | tf_op jit(solution)/shard_map/reduce_sum | solution.py:42
  42.2 1.1 add_convert_fusion.1
  43.3 0.2 all-gather.10.cloned.1.call-start
  43.5 20.7 %all-gather.8.cloned.1.call-done = bf16[4,2304,128]{2,1,0:T(8,128)(2,1)} async-done(((bf16[1,2304,128]{2,1,0:T(8,128)(2,1)}), bf16[4,2304,128]{2,1,0:T(8,128)(2,1)}) %all-gather.8.cloned.1.call-update) | async-done | bytes 2359312 | tf_op jit(solution)/shard_map/all_gather | solution.py:87
  64.2 4.6 %convert_reduce_fusion.4 = (f32[2304,128]{1,0:T(8,128)}, f32[2304,128]{1,0:T(8,128)S(1)}) fusion(bf16[4,2304,128]{2,1,0:T(8,128)(2,1)} %all-gather.8.cloned.1.call-done), kind=kLoop, calls=%fused_computation.5 | loop fusion | flops 5308416 | bytes 4718592 | tf_op jit(solution)/shard_map/reduce_sum | solution.py:42
  68.8 0.4 copy.50
  69.1 1.6 copy.51
  70.8 2.2 add_convert_fusion.2
  73.1 16.7 %all-gather.16.cloned.1.call-done = bf16[4,128,2304]{2,1,0:T(8,128)(2,1)} async-done(((bf16[1,128,2304]{2,1,0:T(8,128)(2,1)}), bf16[4,128,2304]{2,1,0:T(8,128)(2,1)}) %all-gather.16.cloned.1.call-update) | async-done | bytes 2359312 | tf_op jit(solution)/shard_map/all_gather | solution.py:89
  89.8 3.6 %convert_reduce_fusion = (f32[128,2304]{1,0:T(8,128)S(1)}, f32[128,2304]{1,0:T(8,128)S(1)}) fusion(bf16[4,128,2304]{2,1,0:T(8,128)(2,1)} %all-gather.16.cloned.1.call-done), kind=kLoop, calls=%fused_computation.1 | loop fusion | flops 5308416 | bytes 4718592 | tf_op jit(solution)/shard_map/reduce_sum | solution.py:42
  93.5 1.1 add_convert_fusion
  94.7 19.3 %all-gather.14.cloned.1.call-done = bf16[2,4608,64]{1,2,0:T(8,128)(2,1)} async-done(((bf16[2,2304,64]{1,2,0:T(8,128)(2,1)}), bf16[2,4608,64]{1,2,0:T(8,128)(2,1)}) %all-gather.14.cloned.1.call-update) | async-done | bytes 1179664 | tf_op jit(solution)/shard_map/all_gather | solution.py:98
  114.0 1.8 fusion.42
  115.8 1.6 collective-permute-start
  117.3 0.6 fusion.14
  117.9 0.6 collective-permute-start.1
  118.5 19.6 %all-gather.10.cloned.1.call-done = bf16[4608,128]{0,1:T(8,128)(2,1)} async-done(((bf16[2304,128]{0,1:T(8,128)(2,1)}), bf16[4608,128]{0,1:T(8,128)(2,1)}) %all-gather.10.cloned.1.call-update) | async-done | bytes 1179664 | tf_op jit(solution)/shard_map/all_gather | solution.py:97
  138.2 1.8 fusion.40
  140.0 0.2 fusion.28
  140.3 16.4 %all_gather.31 = bf16[1024,128]{0,1:T(8,128)(2,1)S(1)} all-gather(bf16[128,128]{0,1:T(8,128)(2,1)S(1)} %pad_maximum_fusion), channel_id=1, replica_groups=mesh['task'=4,'tensor'=4,'dp'=2] {'task','dp'}, dimensions={0}, use_global_device_ids=true | all-gather | bytes 294912 | tf_op jit(solution)/shard_map/all_gather | solution.py:135
  156.7 17.9 %all_gather.32 = bf16[1024,128]{0,1:T(8,128)(2,1)S(1)} all-gather(bf16[128,128]{0,1:T(8,128)(2,1)S(1)} %fusion.19), channel_id=1, replica_groups=mesh['task'=4,'tensor'=4,'dp'=2] {'task','dp'}, dimensions={0}, use_global_device_ids=true | all-gather | bytes 294912 | tf_op jit(solution)/shard_map/all_gather | solution.py:136
  174.6 0.4 fusion.43
  175.1 3.1 convolution_convert_fusion
  178.2 0.2 convert_element_type.132
  178.5 29.1 %reduce-scatter.2.cloned.1.call-done = bf16[32,4608]{1,0:T(8,128)(2,1)} async-done(((bf16[128,4608]{1,0:T(8,128)(2,1)}), bf16[32,4608]{1,0:T(8,128)(2,1)}) %reduce-scatter.2.cloned.1.call-update) | async-done | bytes 294928 | tf_op jit(solution)/shard_map/reduce_scatter | solution.py:155
  207.6 1.2 fusion.11
  208.9 1.3 multiply_reduce_fusion.1
  210.2 0.9 multiply_convert_fusion.1
  211.2 0.1 eq.126
  211.4 0.1 convert_element_type.168
  211.5 0.6 convert_reduce_fusion.6
  212.1 79.2 %all-gather.20.cloned.1.call-done = bf16[1024,4608]{1,0:T(8,128)(2,1)} async-done(((bf16[32,4608]{1,0:T(8,128)(2,1)}), bf16[1024,4608]{1,0:T(8,128)(2,1)}) %all-gather.20.cloned.1.call-update) | async-done | bytes 9437200 | tf_op jit(solution)/shard_map/all_gather | solution.py:163
  291.3 14.4 %exponential_reduce_fusion = (f32[1024]{0:T(1024)S(1)}, f32[1024]{0:T(1024)S(1)}) fusion(s32[896]{0:T(1024)S(1)} %iota_add_fusion, s32[1024]{0:T(1024)S(1)} %eq.126, bf16[1024,4608]{1,0:T(8,128)(2,1)} %all-gather.20.cloned.1.call-done, bf16[896,4608]{1,0:T(8,128)(2,1)} %param.35), kind=kOutput, calls=%fused_computation.8 | convolution fusion | flops 8461219840 | bytes 17710592 | tf_op jit(solution)/shard_map/dot_general | solution.py:170
  305.7 20.1 %all-reduce = (f32[1024]{0:T(1024)S(1)}, f32[1024]{0:T(1024)S(1)}) all-reduce(f32[1024]{0:T(1024)S(1)} %get-tuple-element.3, f32[1024]{0:T(1024)S(1)} %get-tuple-element.2), channel_id=1, replica_groups=mesh['task'=4,'tensor'=4,'dp'=2] {'tensor','dp'}, use_global_device_ids=true, to_apply=%region_15.16 | all-reduce | flops 2048 | bytes 16384 | tf_op jit(solution)/shard_map/psum | solution.py:182
  325.8 6.1 %all-reduce.1 = (f32[1024]{0:T(1024)S(1)}, f32[1024]{0:T(1024)S(1)}) all-reduce(f32[1024]{0:T(1024)S(1)} %get-tuple-element.10, f32[1024]{0:T(1024)S(1)} %get-tuple-element.11), channel_id=1, replica_groups=mesh['task'=4,'tensor'=4,'dp'=2] {'task'}, use_global_device_ids=true, to_apply=%region_16.17 | all-reduce | flops 2048 | bytes 16384 | tf_op jit(solution)/shard_map/psum | solution.py:181
  332.0 0.7 fusion.41
  332.8 0.6 dynamic_slice.7
  333.4 1.8 pad_maximum_fusion.1
  (76 shorter events, 1.3 us)
Async XLA Ops:
  7.2 4.5 %copy-start.11 = (s32[36,2]{0,1:T(2,128)S(1)}, s32[36,2]{0,1:T(2,128)}, u32[]{:S(2)}) copy-start(s32[36,2]{0,1:T(2,128)} %param.30) | copy-start | bytes 868
  7.2 31.3 %all-gather.12.cloned.1.call-start = ((), (), s32[]{:S(2)}) async-start(), calls=%async_computation.3 | async-start | bytes 2949120 | tf_op jit(solution)/shard_map/all_gather | solution.py:88
  11.6 52.6 %all-gather.8.cloned.1.call-start = ((), (), s32[]{:S(2)}) async-start(), calls=%async_computation.1 | async-start | bytes 2949120 | tf_op jit(solution)/shard_map/all_gather | solution.py:87
  13.7 0.7 copy-start.15
  14.4 1.1 copy-start.4
  16.3 1.2 copy-start.12
  17.5 72.3 %all-gather.16.cloned.1.call-start = ((), (), s32[]{:S(2)}) async-start(), calls=%async_computation.5 | async-start | bytes 2949120 | tf_op jit(solution)/shard_map/all_gather | solution.py:89
  19.6 0.7 copy-start.16
  20.3 1.1 copy-start.6
  21.4 1.5 copy-start.5
  22.7 1.3 copy-start
  22.8 91.2 %all-gather.14.cloned.1.call-start = ((), (), s32[]{:S(2)}) async-start(), calls=%async_computation.4 | async-start | bytes 1769472 | tf_op jit(solution)/shard_map/all_gather | solution.py:98
  24.3 17.8 %copy-start.2 = (bf16[2,2304,64]{1,2,0:T(8,128)(2,1)S(1)}, bf16[2,2304,64]{1,2,0:T(8,128)(2,1)}, u32[]{:S(2)}) copy-start(bf16[2,2304,64]{1,2,0:T(8,128)(2,1)} %param.22) | copy-start | bytes 1769476
  43.3 94.9 %all-gather.10.cloned.1.call-start = ((), (), s32[]{:S(2)}) async-start(), calls=%async_computation.2 | async-start | bytes 1769472 | tf_op jit(solution)/shard_map/all_gather | solution.py:97
  73.0 102.1 %all-gather.18.cloned.1.call-start = ((), (), s32[]{:S(2)}) async-start(), calls=%async_computation.6 | async-start | bytes 1769472 | tf_op jit(solution)/shard_map/all_gather | solution.py:99
  73.1 20.4 %copy-start.3 = (bf16[128,2304]{1,0:T(8,128)(2,1)S(1)}, bf16[128,2304]{1,0:T(8,128)(2,1)}, u32[]{:S(2)}) copy-start(bf16[128,2304]{1,0:T(8,128)(2,1)} %param.23) | copy-start | bytes 1769476
  93.4 20.5 %copy-start.14 = (f32[4608]{0:T(1024)S(1)}, f32[4608]{0:T(1024)}, u32[]{:S(2)}) copy-start(f32[4608]{0:T(1024)} %param.20) | copy-start | bytes 55300
  94.6 113.0 %reduce-scatter.2.cloned.1.call-start = ((), (), s32[]{:S(2)}) async-start(), calls=%async_computation.7 | async-start | bytes 1474560 | tf_op jit(solution)/shard_map/reduce_scatter | solution.py:155
  114.0 3.3 copy-start.13
  115.8 24.2 %collective-permute-start = (bf16[128,64]{0,1:T(8,128)(2,1)S(1)}, bf16[128,64]{0,1:T(8,128)(2,1)S(1)}, u32[]{:S(2)}, u32[]{:S(2)}) collective-permute-start(bf16[128,64]{0,1:T(8,128)(2,1)S(1)} %get-tuple-element.22), channel_id=1, source_target_pairs={{0,2},{2,0},{4,6},{6,4},{1,3},{3,1},{5,7},{7,5},{8,10},{10,8},{12,... | collective-permute-start | bytes 49160 | tf_op jit(solution)/shard_map/ppermute | solution.py:21
  117.9 38.8 %collective-permute-start.1 = (bf16[128,64]{0,1:T(8,128)(2,1)S(1)}, bf16[128,64]{0,1:T(8,128)(2,1)S(1)}, u32[]{:S(2)}, u32[]{:S(2)}) collective-permute-start(bf16[128,64]{0,1:T(8,128)(2,1)S(1)} %fusion.14), channel_id=1, source_target_pairs={{0,2},{2,0},{4,6},{6,4},{1,3},{3,1},{5,7},{7,5},{8,10},{10,8},{12,... | collective-permute-start | bytes 49160 | tf_op jit(solution)/shard_map/ppermute | solution.py:21
  178.2 113.2 %all-gather.20.cloned.1.call-start = ((), (), s32[]{:S(2)}) async-start(), calls=%async_computation.8 | async-start | bytes 9732096 | tf_op jit(solution)/shard_map/all_gather | solution.py:163
  178.5 31.7 %copy-start.7 = (f32[4608]{0:T(1024)S(1)}, f32[4608]{0:T(1024)}, u32[]{:S(2)}) copy-start(f32[4608]{0:T(1024)} %param.33) | copy-start | bytes 55300
  178.5 31.7 %copy-start.8 = (f32[4608]{0:T(1024)S(1)}, f32[4608]{0:T(1024)}, u32[]{:S(2)}) copy-start(f32[4608]{0:T(1024)} %param.34) | copy-start | bytes 55300
  207.6 2.5 copy-start.1
  208.8 2.3 copy-start.10
  208.8 2.5 copy-start.9
Sparse Core Ops, SparseCore 0:
  11.7 26.7 all-gather.11
  40.1 24.0 all-gather.7
  65.7 24.0 all-gather.15
  91.2 22.7 all-gather.13
  115.4 22.7 all-gather.9
  139.6 24.4 all-gather.17
  178.3 29.2 reduce-scatter.1
  211.2 80.0 all-gather.19
